TPU v7x, 128 devices: a whole 4x4x4 slice. The times are simulated.
128 devices in a mesh: orig: 8 (over x, core), dest: 16 (over y, z).
Axes of the slice: x: 4, y: 4, z: 4, core: 2. Of those that a mesh axis runs over, the one named last changes fastest.
Arguments:
- root_blocks: bfloat16 [1024, 1024, 1024], P(('orig', 'dest')), may hold values from 0.0099487305 to 1
- sector_map: int32 [1024], replicated, may hold values from 0 to 127
- dest_owner: int32 [1024, 1], P(('orig', 'dest')), may hold values from 0 to 15; in each aligned block of 8 rows (0 to 7, 8 to 15, ...) at most 2 rows name the same one
- local_row: int32 [1024], P(('orig', 'dest')), may hold values from 0 to 7
- local_col: int32 [1024], P(('orig', 'dest')), may hold values from 0 to 3
- present: int32 [1024], P(('orig', 'dest')), may hold values 0 or 1
- prior: float32 [8192, 8192], P('orig', 'dest'), may hold values from 1 to 30
- row_target: float32 [8192], P('orig'), may hold values from 4096 to 16384
- col_target: float32 [8192], P('dest'), may hold values from 4096 to 16384
Outputs:
- balanced: float32 [8192, 8192], P('orig', 'dest')
Inputs may be any that keep to these rules, and one draw needn't show every extreme that they name: Among the 8 root blocks of one device, no value of dest_owner occurs more than 2 times; some device has one that occurs exactly 2 times.
All inputs are finite; a program needn't handle non-finite values. No bound on the sum of `present` on one device may be relied on, other than what follows from the above.
Results may differ from a plain program's by a relative error of at most 0.0003.
Values sent between devices are 32-bit elements; how exact they have to be, the bound alone decides.
A program may use at most 128 MiB of HBM per device.

v0:
```python
import jax
import jax.numpy as jnp
from jax import lax
from jax.sharding import PartitionSpec as P

S_T = 128


def shards(
    root_blocks,
    sector_map,
    dest_owner,
    local_row,
    local_col,
    present,
    prior,
    row_target,
    col_target,
):
    n_dest = lax.axis_size("dest")
    rows_here = prior.shape[0]
    cols_here = prior.shape[1]
    s_t = S_T
    tro = rows_here // s_t
    trd = cols_here // s_t
    highest = lax.Precision.HIGHEST
    concord = (sector_map[:, None] == jnp.arange(s_t, dtype=jnp.int32)[None, :]).astype(
        jnp.bfloat16
    )
    concord_wide = concord.astype(jnp.float32)
    left = jnp.einsum("sk,bsj->bkj", concord, root_blocks, preferred_element_type=jnp.float32)
    aggregated = jnp.einsum(
        "bkj,jl->bkl", left, concord_wide, preferred_element_type=jnp.float32, precision=highest
    )
    aggregated = aggregated * present.astype(jnp.float32)[:, None, None]
    owner = dest_owner[:, 0]
    target_local = local_row * trd + local_col
    global_slot = owner * (tro * trd) + target_local
    picker = (
        jnp.arange(n_dest * tro * trd, dtype=jnp.int32)[:, None] == global_slot[None, :]
    ).astype(jnp.float32)
    dense = jnp.einsum(
        "pb,bkl->pkl", picker, aggregated, preferred_element_type=jnp.float32, precision=highest
    )
    received = lax.psum_scatter(dense, "dest", scatter_dimension=0, tiled=True)
    added = received.reshape(tro, trd, s_t, s_t).transpose(0, 2, 1, 3).reshape(rows_here, cols_here)
    table = prior + added
    row_sums = lax.psum(jnp.sum(table, axis=1), "dest")
    row_factor = row_target / row_sums
    scaled = table * row_factor[:, None]
    col_sums = lax.psum(jnp.sum(scaled, axis=0), "orig")
    col_factor = col_target / col_sums
    return scaled * col_factor[None, :]


def solution(mesh):
    placed = (
        P(("orig", "dest"), None, None),
        P(),
        P(("orig", "dest"), None),
        P(("orig", "dest")),
        P(("orig", "dest")),
        P(("orig", "dest")),
        P("orig", "dest"),
        P("orig"),
        P("dest"),
    )
    return jax.shard_map(
        shards, mesh=mesh, in_specs=placed, out_specs=P("orig", "dest"), check_vma=False
    )
```

profile of v0, /device:TPU:1, one launch (start us, length us, event | category | flops | bytes accessed | tf_op | source)
XLA Modules:
  0.0 301.5 jit_solution(12025145763176269876)
XLA Ops:
  6.5 0.0 reduce-scatter.2.cloned.1.call-start
  6.5 0.7 convert_element_type.2
  7.2 0.0 copy-start.1
  7.2 8.7 %fusion.8 = f32[128,8,1024]{2,0,1:T(8,128)S(1)} fusion(bf16[8,1024,1024]{2,1,0:T(8,128)(2,1)} %param.9, s32[1024]{0:T(1024)} %param.10), kind=kOutput, calls=%fused_computation.9 | convolution fusion | flops 2147614720 | bytes 20975616 | tf_op jit(solution)/shard_map/sk,bsj->bkj/dot_general | solution.py:31
  15.9 0.0 copy-done.1
  15.9 0.0 copy-start.4
  15.9 0.0 copy-start.5
  15.9 0.0 copy-start.6
  16.0 4.3 %fusion.3 = f32[8,128,128]{2,0,1:T(8,128)S(1)} fusion(f32[128,8,1024]{2,0,1:T(8,128)S(1)} %fusion.8, f32[8]{0:T(128)S(1)} %convert_element_type.2, s32[1024]{0:T(1024)S(1)} %copy-done.1), kind=kOutput, calls=%fused_computation.6 | convolution fusion | flops 1610874880 | bytes 4722720 | tf_op jit(solution)/shard_map/bkj,jl->bkl/dot_general | solution.py:32
  20.2 0.0 copy-done.4
  20.3 0.0 copy-done.5
  20.3 0.0 copy-done.6
  20.3 17.4 %fusion.13 = f32[512,128,128]{2,0,1:T(8,128)} fusion(f32[8,128,128]{2,0,1:T(8,128)S(1)} %fusion.3, s32[8]{0:T(128)S(1)} %bitcast_add_fusion.1), kind=kOutput, calls=%fused_computation.14 | convolution fusion | flops 805310464 | bytes 34078752 | tf_op jit(solution)/shard_map/pb,bkl->pkl/dot_general | solution.py:42
  37.7 0.0 reduce-scatter.2.cloned.1.call-update
  37.7 198.4 %reduce-scatter.2.cloned.1.call-done = f32[32,128,128]{2,0,1:T(8,128)} async-done(((f32[512,128,128]{2,0,1:T(8,128)}), f32[32,128,128]{2,0,1:T(8,128)}) %reduce-scatter.2.cloned.1.call-update) | async-done | bytes 2097168 | tf_op jit(solution)/shard_map/reduce_scatter | solution.py:45
  236.1 0.0 copy-start
  236.1 2.1 copy.10
  238.2 0.1 copy-done
  238.3 0.0 copy-start.2
  238.3 0.3 fusion.16
  238.6 31.1 %psum.14 = f32[1024]{0:T(1024)S(1)} all-reduce(f32[1024]{0:T(1024)S(1)} %fusion.16), channel_id=1, replica_groups=mesh['orig'=8,'dest'=16] {'dest'}, use_global_device_ids=true, to_apply=%region_2.0 | all-reduce | flops 1024 | bytes 8192 | tf_op jit(solution)/shard_map/psum | solution.py:48
  269.7 0.0 copy-done.2
  269.7 0.0 copy-start.3
  269.7 1.9 multiply_reduce_fusion
  271.6 19.9 %psum.15 = f32[512]{0:T(512)S(1)} all-reduce(f32[512]{0:T(512)S(1)} %multiply_reduce_fusion), channel_id=1, replica_groups=mesh['orig'=8,'dest'=16] {'orig'}, use_global_device_ids=true, to_apply=%region_4.0 | all-reduce | flops 512 | bytes 4096 | tf_op jit(solution)/shard_map/psum | solution.py:51
  291.4 0.0 copy-done.3
  291.4 3.2 %multiply_multiply_fusion = f32[1024,512]{1,0:T(8,128)} fusion(f32[512]{0:T(512)S(1)} %div.7, f32[1024]{0:T(1024)S(1)} %div.6, f32[1024,512]{1,0:T(8,128)} %param.15, f32[128,8,4,128]{3,2,1,0:T(4,128)S(1)} %bitcast.31), kind=kLoop, calls=%fused_computation.4 | loop fusion | flops 1572864 | bytes 6297600 | tf_op jit(solution)/shard_map/mul | solution.py:53
  (3 shorter events, 0.0 us)
Async XLA Ops:
  6.5 229.6 %reduce-scatter.2.cloned.1.call-start = ((), (), s32[]{:S(2)}) async-start(), calls=%async_computation.1 | async-start | bytes 35651584 | tf_op jit(solution)/shard_map/reduce_scatter | solution.py:45
  7.2 8.7 %copy-start.1 = (s32[1024]{0:T(1024)S(1)}, s32[1024]{0:T(1024)}, u32[]{:S(2)}) copy-start(s32[1024]{0:T(1024)} %param.10) | copy-start | bytes 12292
  15.9 4.3 %copy-start.4 = (s32[8]{0:T(128)S(1)}, s32[8]{0:T(128)}, u32[]{:S(2)}) copy-start(s32[8]{0:T(128)} %param.13) | copy-start | bytes 100
  15.9 4.3 %copy-start.5 = (s32[8]{0:T(128)S(1)}, s32[8]{0:T(128)}, u32[]{:S(2)}) copy-start(s32[8]{0:T(128)} %param.12) | copy-start | bytes 100
  15.9 4.3 %copy-start.6 = (s32[8,1]{0,1:T(1,128)S(1)}, s32[8,1]{0,1:T(1,128)}, u32[]{:S(2)}) copy-start(s32[8,1]{0,1:T(1,128)} %param.11) | copy-start | bytes 100
  236.1 2.2 copy-start
  238.3 31.4 %copy-start.2 = (f32[1024]{0:T(1024)S(1)}, f32[1024]{0:T(1024)}, u32[]{:S(2)}) copy-start(f32[1024]{0:T(1024)} %param.16) | copy-start | bytes 12292
  269.7 21.7 %copy-start.3 = (f32[512]{0:T(512)S(1)}, f32[512]{0:T(512)}, u32[]{:S(2)}) copy-start(f32[512]{0:T(512)} %param.17) | copy-start | bytes 6148
Sparse Core Ops, SparseCore 0:
  37.8 198.2 reduce-scatter.1
where the time goes:
time: 302 us; the launch traced here: 301 us
  waiting for transfers between devices  198 us (66%)
  blocking collectives  51 us (17%)
  matrix products  30.4 us (10%)
  between operations  13.5 us (4%)
  other arithmetic  6 us (2%)
    reduce_scatter x1, waiting for transfers between devices, shards(): received = lax.psum_scatter(dense, 'dest', scatter_dimension=0, tiled=True)  198 us
    psum x1, blocking collectives, shards(): row_sums = lax.psum(jnp.sum(table, axis=1), 'dest')  31.1 us
    psum x1, blocking collectives, shards(): col_sums = lax.psum(jnp.sum(scaled, axis=0), 'orig')  19.9 us
    dot_general x1, matrix products, shards(): jnp.einsum('pb,bkl->pkl', picker, aggregated, preferred_element_type=jnp....  17.4 us
    dot_general x1, matrix products, shards(): jnp.einsum('sk,bsj->bkj', concord, root_blocks, preferred_element_type=jn...  8.7 us
  transfers between devices with their start and end apart: 1, of which 1 were waited for; matrix products, arithmetic and copies ran while one was open for 0% of the time, Pallas kernels for 0%

commit v1 on v0

--- a/solution.py
+++ b/solution.py
@@ -48,7 +48,7 @@
     row_sums = lax.psum(jnp.sum(table, axis=1), "dest")
     row_factor = row_target / row_sums
     scaled = table * row_factor[:, None]
-    col_sums = lax.psum(jnp.sum(scaled, axis=0), "orig")
+    col_sums = jnp.sum(lax.all_gather(jnp.sum(scaled, axis=0), "orig"), axis=0)
     col_factor = col_target / col_sums
     return scaled * col_factor[None, :]
 

time: 302 us -> 302 us (level)
    psum x1 -> x0, blocking collectives: 19.9 us -> none  [shards(): col_sums = lax.psum(jnp.sum(scaled, axis=0), 'orig')]
    all_gather x0 -> x1, blocking collectives: none -> 19.7 us  [shards(): col_sums = jnp.sum(lax.all_gather(jnp.sum(scaled, axis=0), 'orig'), axis=0)]
where the time goes in v1:
time: 302 us; the launch traced here: 301 us
  waiting for transfers between devices  198 us (66%)
  blocking collectives  50.9 us (17%)
  matrix products  30.4 us (10%)
  between operations  13.5 us (4%)
  other arithmetic  6.03 us (2%)
    reduce_scatter x1, waiting for transfers between devices, shards(): received = lax.psum_scatter(dense, 'dest', scatter_dimension=0, tiled=True)  198 us
    psum x1, blocking collectives, shards(): row_sums = lax.psum(jnp.sum(table, axis=1), 'dest')  31.1 us
    all_gather x1, blocking collectives, shards(): col_sums = jnp.sum(lax.all_gather(jnp.sum(scaled, axis=0), 'orig'), axis=0)  19.7 us
    dot_general x1, matrix products, shards(): jnp.einsum('pb,bkl->pkl', picker, aggregated, preferred_element_type=jnp....  17.4 us
    dot_general x1, matrix products, shards(): jnp.einsum('sk,bsj->bkj', concord, root_blocks, preferred_element_type=jn...  8.7 us
  transfers between devices with their start and end apart: 1, of which 1 were waited for; matrix products, arithmetic and copies ran while one was open for 0% of the time, Pallas kernels for 0%

profile of v1, /device:TPU:1, one launch (start us, length us, event | category | flops | bytes accessed | tf_op | source)
XLA Modules:
  0.0 301.4 jit_solution(403991469259357759)
XLA Ops:
  6.5 0.0 reduce-scatter.2.cloned.1.call-start
  6.5 0.7 convert_element_type.2
  7.2 0.0 copy-start.1
  7.2 8.7 %fusion.8 = f32[128,8,1024]{2,0,1:T(8,128)S(1)} fusion(bf16[8,1024,1024]{2,1,0:T(8,128)(2,1)} %param.9, s32[1024]{0:T(1024)} %param.10), kind=kOutput, calls=%fused_computation.9 | convolution fusion | flops 2147614720 | bytes 20975616 | tf_op jit(solution)/shard_map/sk,bsj->bkj/dot_general | solution.py:31
  15.9 0.0 copy-done.1
  15.9 0.0 copy-start.4
  15.9 0.0 copy-start.5
  15.9 0.0 copy-start.6
  16.0 4.3 %fusion.3 = f32[8,128,128]{2,0,1:T(8,128)S(1)} fusion(f32[128,8,1024]{2,0,1:T(8,128)S(1)} %fusion.8, f32[8]{0:T(128)S(1)} %convert_element_type.2, s32[1024]{0:T(1024)S(1)} %copy-done.1), kind=kOutput, calls=%fused_computation.6 | convolution fusion | flops 1610874880 | bytes 4722720 | tf_op jit(solution)/shard_map/bkj,jl->bkl/dot_general | solution.py:32
  20.2 0.0 copy-done.4
  20.3 0.0 copy-done.5
  20.3 0.0 copy-done.6
  20.3 17.4 %fusion.13 = f32[512,128,128]{2,0,1:T(8,128)} fusion(f32[8,128,128]{2,0,1:T(8,128)S(1)} %fusion.3, s32[8]{0:T(128)S(1)} %bitcast_add_fusion.1), kind=kOutput, calls=%fused_computation.14 | convolution fusion | flops 805310464 | bytes 34078752 | tf_op jit(solution)/shard_map/pb,bkl->pkl/dot_general | solution.py:42
  37.7 0.0 reduce-scatter.2.cloned.1.call-update
  37.7 198.4 %reduce-scatter.2.cloned.1.call-done = f32[32,128,128]{2,0,1:T(8,128)} async-done(((f32[512,128,128]{2,0,1:T(8,128)}), f32[32,128,128]{2,0,1:T(8,128)}) %reduce-scatter.2.cloned.1.call-update) | async-done | bytes 2097168 | tf_op jit(solution)/shard_map/reduce_scatter | solution.py:45
  236.1 0.0 copy-start
  236.1 2.1 copy.11
  238.2 0.1 copy-done
  238.3 0.0 copy-start.2
  238.3 0.3 fusion.16
  238.6 31.1 %psum.7 = f32[1024]{0:T(1024)S(1)} all-reduce(f32[1024]{0:T(1024)S(1)} %fusion.16), channel_id=1, replica_groups=mesh['orig'=8,'dest'=16] {'dest'}, use_global_device_ids=true, to_apply=%region_2.0 | all-reduce | flops 1024 | bytes 8192 | tf_op jit(solution)/shard_map/psum | solution.py:48
  269.7 0.0 copy-done.2
  269.7 0.0 copy-start.3
  269.7 1.9 multiply_reduce_fusion
  271.6 19.7 %all-gather.1 = f32[8,1,512]{2,1,0:T(1,128)S(1)} all-gather(f32[1,1,512]{2,1,0:T(1,128)S(1)} %bitcast.34), channel_id=2, replica_groups=mesh['orig'=8,'dest'=16] {'orig'}, dimensions={0}, use_global_device_ids=true | all-gather | bytes 18432 | tf_op jit(solution)/shard_map/all_gather | solution.py:51
  291.4 0.0 copy-done.3
  291.4 3.2 %multiply_multiply_fusion = f32[1024,512]{1,0:T(8,128)} fusion(f32[512]{0:T(512)S(1)} %div.7, f32[1024]{0:T(1024)S(1)} %div.6, f32[1024,512]{1,0:T(8,128)} %param.15, f32[128,8,4,128]{3,2,1,0:T(4,128)S(1)} %bitcast.32), kind=kLoop, calls=%fused_computation.4 | loop fusion | flops 1572864 | bytes 6297600 | tf_op jit(solution)/shard_map/mul | solution.py:53
  (4 shorter events, 0.0 us)
Async XLA Ops:
  6.5 229.6 %reduce-scatter.2.cloned.1.call-start = ((), (), s32[]{:S(2)}) async-start(), calls=%async_computation.1 | async-start | bytes 35651584 | tf_op jit(solution)/shard_map/reduce_scatter | solution.py:45
  7.2 8.7 %copy-start.1 = (s32[1024]{0:T(1024)S(1)}, s32[1024]{0:T(1024)}, u32[]{:S(2)}) copy-start(s32[1024]{0:T(1024)} %param.10) | copy-start | bytes 12292
  15.9 4.3 %copy-start.4 = (s32[8]{0:T(128)S(1)}, s32[8]{0:T(128)}, u32[]{:S(2)}) copy-start(s32[8]{0:T(128)} %param.13) | copy-start | bytes 100
  15.9 4.3 %copy-start.5 = (s32[8]{0:T(128)S(1)}, s32[8]{0:T(128)}, u32[]{:S(2)}) copy-start(s32[8]{0:T(128)} %param.12) | copy-start | bytes 100
  15.9 4.3 %copy-start.6 = (s32[8,1]{0,1:T(1,128)S(1)}, s32[8,1]{0,1:T(1,128)}, u32[]{:S(2)}) copy-start(s32[8,1]{0,1:T(1,128)} %param.11) | copy-start | bytes 100
  236.1 2.2 copy-start
  238.3 31.4 %copy-start.2 = (f32[1024]{0:T(1024)S(1)}, f32[1024]{0:T(1024)}, u32[]{:S(2)}) copy-start(f32[1024]{0:T(1024)} %param.16) | copy-start | bytes 12292
  269.7 21.7 %copy-start.3 = (f32[512]{0:T(512)S(1)}, f32[512]{0:T(512)}, u32[]{:S(2)}) copy-start(f32[512]{0:T(512)} %param.17) | copy-start | bytes 6148
Sparse Core Ops, SparseCore 0:
  37.8 198.2 reduce-scatter.1
